TPU v7x, 32 devices: a whole 2x2x4 slice. The times are simulated.
32 devices in a mesh: row: 8 (over z, core), col: 4 (over y, x).
Axes of the slice: x: 2, y: 2, z: 4, core: 2. Of those that a mesh axis runs over, the one named last changes fastest.
Arguments:
- context: bfloat16 [128, 16384], P('row', 'col'), may hold values from -6 to 6
- out_weight: bfloat16 [16384, 16384], P('col', 'row'), may hold values from -0.046875 to 0.046875
- residual: bfloat16 [128, 16384], P('col', 'row'), may hold values from -80 to 80
- teacher_gain: float32 [16384], replicated, may hold values from 0.5 to 1.5
- student_hidden: bfloat16 [128, 4096], P(('row', 'col')), may hold values from -6 to 6
- student_gain: float32 [4096], replicated, may hold values from 0.5 to 1.5
- projector: bfloat16 [4096, 16384], P(None, ('row', 'col')), may hold values from -0.09375 to 0.09375
Outputs:
- grad_proj: float32 [4096, 16384], P(None, ('row', 'col'))
- grad_gain: float32 [4096], replicated
- loss: float32 [], replicated
All inputs are finite; a program needn't handle non-finite values.
Results may differ from a plain program's by a relative error of at most 0.0065.
Values may be sent and summed in bfloat16 or wider, within the bound.
A program may use at most 64 MiB of HBM per device.

v0:
```python
import jax
import jax.numpy as jnp
from jax import lax
from jax.sharding import PartitionSpec as P

D_T = 16384
norm_eps = 1e-05


def normalize(hidden):
    widened = hidden.astype(jnp.float32)
    return widened * lax.rsqrt(jnp.mean(widened * widened, axis=1, keepdims=True) + norm_eps)


def per_device(
    context, out_weight, residual, teacher_gain, student_hidden, student_gain, projector
):
    row_index = lax.axis_index("row")
    context_all = lax.all_gather(context, "row", axis=0, tiled=True)
    out_block = out_weight.shape[1]
    summed = lax.psum_scatter(
        jnp.dot(context_all, out_weight, preferred_element_type=jnp.float32),
        "col",
        scatter_dimension=0,
        tiled=True,
    )
    summed = summed + residual.astype(jnp.float32)
    squares = lax.psum(jnp.sum(summed * summed, axis=1), "row")
    gain_block = lax.dynamic_slice_in_dim(teacher_gain, row_index * out_block, out_block)
    final_rows = (summed * lax.rsqrt(squares / D_T + norm_eps)[:, None] * gain_block).astype(
        jnp.bfloat16
    )
    target = lax.all_to_all(final_rows, "col", split_axis=1, concat_axis=0, tiled=True)
    hidden_all = lax.all_gather(student_hidden, ("row", "col"), axis=0, tiled=True)
    normed_all = normalize(hidden_all)
    student_all = (normed_all * student_gain).astype(jnp.bfloat16)
    predicted = jnp.dot(student_all, projector, preferred_element_type=jnp.float32)
    difference = predicted - target.astype(jnp.float32)
    loss_part = jnp.sum(difference * difference)
    loss_total = lax.psum(loss_part, ("row", "col"))
    error_term = (difference * (1.0 / 64.0)).astype(jnp.bfloat16)
    grad_proj = lax.dot_general(
        student_all, error_term, (((0,), (0,)), ((), ())), preferred_element_type=jnp.float32
    )
    grad_normed = lax.dot_general(
        error_term, projector, (((1,), (1,)), ((), ())), preferred_element_type=jnp.float32
    )
    gain_part = jnp.sum(grad_normed * normed_all, axis=0)
    grad_gain = lax.psum(gain_part, ("row", "col"))
    tokens_all = predicted.shape[0]
    loss = loss_total / (tokens_all * D_T)
    return (grad_proj, grad_gain, loss)


def solution(mesh):
    placed = (
        P("row", "col"),
        P("col", "row"),
        P("col", "row"),
        P(),
        P(("row", "col"), None),
        P(),
        P(None, ("row", "col")),
    )
    return jax.shard_map(
        per_device,
        mesh=mesh,
        in_specs=placed,
        out_specs=(P(None, ("row", "col")), P(), P()),
        check_vma=False,
    )
```

profile of v0, /device:TPU:12, one launch (start us, length us, event | category | flops | bytes accessed | tf_op | source)
XLA Modules:
  0.0 205.2 jit_solution(2190091404144003150)
XLA Ops:
  7.2 0.0 all-gather.4.cloned.1.call-start
  7.2 0.7 all-gather.4.cloned.1.call-update
  7.9 0.0 all-gather.6.cloned.1.call-start
  7.9 0.7 all-gather.6.cloned.1.call-update
  8.6 0.0 reduce-scatter.2.cloned.1.call-start
  8.7 24.4 %all-gather.4.cloned.1.call-done = bf16[128,4096]{1,0:T(8,128)(2,1)} async-done(((bf16[16,4096]{1,0:T(8,128)(2,1)}), bf16[128,4096]{1,0:T(8,128)(2,1)}) %all-gather.4.cloned.1.call-update) | async-done | bytes 1048592 | tf_op jit(solution)/shard_map/all_gather | solution.py:19
  33.1 9.4 %fusion.4 = f32[128,2048]{1,0:T(8,128)} fusion(bf16[128,4096]{1,0:T(8,128)(2,1)} %all-gather.4.cloned.1.call-done, bf16[4096,2048]{1,0:T(8,128)(2,1)} %param.8), kind=kOutput, calls=%fused_computation.16 | convolution fusion | flops 2147483648 | bytes 18874368 | tf_op jit(solution)/shard_map/dot_general | solution.py:22
  42.5 0.0 reduce-scatter.2.cloned.1.call-update
  42.5 0.0 copy-start.1
  42.5 0.0 dynamic-slice-start
  42.5 46.0 %all-gather.6.cloned.1.call-done = bf16[32,4,4096]{2,1,0:T(4,128)(2,1)} async-done(((bf16[1,4,4096]{2,1,0:T(4,128)(2,1)}), bf16[32,4,4096]{2,1,0:T(4,128)(2,1)}) %all-gather.6.cloned.1.call-update) | async-done | bytes 1048592 | tf_op jit(solution)/shard_map/all_gather | solution.py:34
  88.5 1.3 reshape.25
  89.8 0.2 multiply_reduce_fusion
  90.0 29.6 %reduce-scatter.2.cloned.1.call-done = f32[32,2048]{1,0:T(8,128)} async-done(((f32[128,2048]{1,0:T(8,128)}), f32[32,2048]{1,0:T(8,128)}) %reduce-scatter.2.cloned.1.call-update) | async-done | bytes 262160 | tf_op jit(solution)/shard_map/reduce_scatter | solution.py:21
  119.7 1.1 multiply_reduce_fusion.2
  120.8 12.7 %psum.21 = f32[32]{0:T(128)S(1)} all-reduce(f32[32]{0:T(128)S(1)} %multiply_reduce_fusion.2), channel_id=1, replica_groups=mesh['row'=8,'col'=4] {'row'}, use_global_device_ids=true, to_apply=%region_3.0 | all-reduce | flops 32 | bytes 256 | tf_op jit(solution)/shard_map/psum | solution.py:28
  133.4 1.0 multiply_convert_fusion.2
  134.5 0.7 copy.14
  135.2 3.9 %all-to-all-start = ((bf16[32,4,512]{2,0,1:T(8,128)(2,1)}), bf16[32,4,512]{2,0,1:T(8,128)(2,1)S(1)}, u32[]{:S(2)}, u32[]{:S(2)}) async-start(bf16[32,4,512]{2,0,1:T(8,128)(2,1)} %bitcast.11), calls=%async_computation.1 | async-start | bytes 262144 | tf_op jit(solution)/shard_map/all_to_all | solution.py:33
  139.0 3.9 %all-to-all-done = bf16[32,4,512]{2,0,1:T(8,128)(2,1)S(1)} async-done(((bf16[32,4,512]{2,0,1:T(8,128)(2,1)}), bf16[32,4,512]{2,0,1:T(8,128)(2,1)S(1)}, u32[]{:S(2)}, u32[]{:S(2)}) %all-to-all-start) | async-done | bytes 131104 | tf_op jit(solution)/shard_map/all_to_all | solution.py:33
  143.0 3.7 %multiply_reduce_fusion.1 = (f32[]{:T(128)}, f32[128,512]{1,0:T(8,128)S(1)}) fusion(f32[128,512]{1,0:T(8,128)S(1)} %bitcast.12, bf16[4096,512]{1,0:T(8,128)(2,1)} %param.13, f32[128,4096]{1,0:T(8,128)S(1)} %reshape.25, f32[4096]{0:T(1024)S(1)} %copy-done.2, f32[128]{0:T(128)S(1)} %add_rsqrt_fusion.1), kind=kOutput, calls=%fused_computation.5 | convolution fusion | flops 538640384 | bytes 6832644 | tf_op jit(solution)/shard_map/dot_general | solution.py:37
  146.7 1.5 fusion
  148.2 4.8 %fusion.1 = f32[4096,512]{1,0:T(8,128)} fusion(f32[128,512]{1,0:T(8,128)S(1)} %get-tuple-element.6, f32[128,4096]{1,0:T(8,128)S(1)} %reshape.25, f32[4096]{0:T(1024)S(1)} %copy-done.2, f32[128]{0:T(128)S(1)} %add_rsqrt_fusion.1), kind=kOutput, calls=%fused_computation.11 | convolution fusion | flops 538574848 | bytes 10764800 | tf_op jit(solution)/shard_map/dot_general | solution.py:42
  153.0 43.9 %all-reduce = (f32[4096]{0:T(1024)}, f32[]{:T(128)}) all-reduce(f32[4096]{0:T(1024)S(1)} %fusion, f32[]{:T(128)} %get-tuple-element.5), channel_id=1, replica_groups=mesh['row'=8,'col'=4] {'row','col'}, use_global_device_ids=true, to_apply=%region_5.0 | all-reduce | flops 4097 | bytes 32776 | tf_op jit(solution)/shard_map/psum | solution.py:49
  (9 shorter events, 0.0 us)
Async XLA Ops:
  7.2 25.9 %all-gather.4.cloned.1.call-start = ((), (), s32[]{:S(2)}) async-start(), calls=%async_computation.2 | async-start | bytes 1179648 | tf_op jit(solution)/shard_map/all_gather | solution.py:19
  7.9 80.6 %all-gather.6.cloned.1.call-start = ((), (), s32[]{:S(2)}) async-start(), calls=%async_computation.4 | async-start | bytes 1081344 | tf_op jit(solution)/shard_map/all_gather | solution.py:34
  8.6 111.0 %reduce-scatter.2.cloned.1.call-start = ((), (), s32[]{:S(2)}) async-start(), calls=%async_computation.3 | async-start | bytes 1310720 | tf_op jit(solution)/shard_map/reduce_scatter | solution.py:21
  42.5 77.2 %copy-start.1 = (bf16[32,2048]{1,0:T(8,128)(2,1)S(1)}, bf16[32,2048]{1,0:T(8,128)(2,1)}, u32[]{:S(2)}) copy-start(bf16[32,2048]{1,0:T(8,128)(2,1)} %param.9) | copy-start | bytes 393220
  42.5 90.9 %dynamic-slice-start = ((f32[16384]{0:T(1024)}, s32[]{:T(128)}), f32[2048]{0:T(1024)S(1)}, s32[]{:S(2)}) async-start(f32[16384]{0:T(1024)} %param.10, s32[]{:T(128)} %select_n.3), calls=%async_computation.5 | async-start | bytes 16896 | tf_op jit(solution)/shard_map/dynamic_slice | solution.py:29
  89.8 53.2 %copy-start.2 = (f32[4096]{0:T(1024)S(1)}, f32[4096]{0:T(1024)}, u32[]{:S(2)}) copy-start(f32[4096]{0:T(1024)} %param.12) | copy-start | bytes 49156
  135.2 7.8 %all-to-all-start = ((bf16[32,4,512]{2,0,1:T(8,128)(2,1)}), bf16[32,4,512]{2,0,1:T(8,128)(2,1)S(1)}, u32[]{:S(2)}, u32[]{:S(2)}) async-start(bf16[32,4,512]{2,0,1:T(8,128)(2,1)} %bitcast.11), calls=%async_computation.1 | async-start | bytes 262144 | tf_op jit(solution)/shard_map/all_to_all | solution.py:33
  143.0 3.8 %copy-start = (bf16[4096,512]{1,0:T(8,128)(2,1)S(1)}, bf16[4096,512]{1,0:T(8,128)(2,1)}, u32[]{:S(2)}) copy-start(bf16[4096,512]{1,0:T(8,128)(2,1)} %param.13) | copy-start | bytes 12582916
Sparse Core Ops, SparseCore 0:
  9.6 23.4 all-gather.3
  36.1 52.4 all-gather.5
  92.0 27.6 reduce-scatter.1
where the time goes:
time: 206 us; the launch traced here: 205 us
  waiting for transfers between devices  105 us (51%)
  blocking collectives  56.6 us (27%)
  matrix products  19.4 us (9%)
  between operations  15.6 us (8%)
  starting transfers between devices  3.99 us (2%)
  other arithmetic  2.4 us (1%)
    all_gather x1, waiting for transfers between devices, per_device(): lax.all_gather(student_hidden, ('row', 'col'), axis=0, tiled=True)  46 us
    psum x1, blocking collectives, per_device(): grad_gain = lax.psum(gain_part, ('row', 'col'))  43.9 us
    reduce_scatter x1, waiting for transfers between devices, per_device(): lax.psum_scatter(jnp.dot(context_all, out_weight, preferred_element_type=...  29.6 us
    all_gather x1, waiting for transfers between devices, per_device(): context_all = lax.all_gather(context, 'row', axis=0, tiled=True)  24.4 us
    psum x1, blocking collectives, per_device(): squares = lax.psum(jnp.sum(summed * summed, axis=1), 'row')  12.7 us
    dot_general x1, matrix products, per_device(): jnp.dot(context_all, out_weight, preferred_element_type=jnp.float32)  9.41 us
    dot_general x1, matrix products, per_device(): lax.dot_general(student_all, error_term, (((0,), (0,)), ((), ())), prefer...  4.77 us
  transfers between devices with their start and end apart: 4, of which 4 were waited for; matrix products, arithmetic and copies ran while one was open for 5% of the time, Pallas kernels for 0%

commit v1 on v0

--- a/solution.py
+++ b/solution.py
@@ -46,7 +46,7 @@
         error_term, projector, (((1,), (1,)), ((), ())), preferred_element_type=jnp.float32
     )
     gain_part = jnp.sum(grad_normed * normed_all, axis=0)
-    grad_gain = lax.psum(gain_part, ("row", "col"))
+    grad_gain = lax.psum(lax.psum(gain_part, "col"), "row")
     tokens_all = predicted.shape[0]
     loss = loss_total / (tokens_all * D_T)
     return (grad_proj, grad_gain, loss)

time: 206 us -> 247 us (1.20)
  the two profiles are of different devices: /device:TPU:12 before, /device:TPU:0 now
where the time goes in v1:
time: 247 us
  waiting for transfers between devices  108 us (44%)
  blocking collectives  96.1 us (39%)
  matrix products  19.4 us (8%)
  between operations  15.6 us (6%)
  starting transfers between devices  3.44 us (1%)
    all_gather x1, waiting for transfers between devices, per_device(): lax.all_gather(student_hidden, ('row', 'col'), axis=0, tiled=True)  46.8 us
    psum x2, blocking collectives, per_device(): grad_gain = lax.psum(lax.psum(gain_part, 'col'), 'row')  42.9 us
    psum x1, blocking collectives, per_device(): loss_total = lax.psum(loss_part, ('row', 'col'))  37 us
    reduce_scatter x1, waiting for transfers between devices, per_device(): lax.psum_scatter(jnp.dot(context_all, out_weight, preferred_element_type=...  28.9 us
    all_gather x1, waiting for transfers between devices, per_device(): context_all = lax.all_gather(context, 'row', axis=0, tiled=True)  25.9 us
    psum x1, blocking collectives, per_device(): squares = lax.psum(jnp.sum(summed * summed, axis=1), 'row')  16.2 us
    dot_general x1, matrix products, per_device(): jnp.dot(context_all, out_weight, preferred_element_type=jnp.float32)  9.41 us
    all_to_all x1, waiting for transfers between devices, per_device(): lax.all_to_all(final_rows, 'col', split_axis=1, concat_axis=0, tiled=True)  4.97 us
  transfers between devices with their start and end apart: 4, of which 4 were waited for; matrix products, arithmetic and copies ran while one was open for 4% of the time, Pallas kernels for 0%

profile of v1, /device:TPU:0, one launch (start us, length us, event | category | flops | bytes accessed | tf_op | source)
XLA Modules:
  0.0 246.9 jit_solution(8663760593872334987)
XLA Ops:
  7.2 0.0 all-gather.4.cloned.1.call-start
  7.2 0.7 all-gather.4.cloned.1.call-update
  7.9 0.0 all-gather.6.cloned.1.call-start
  7.9 0.7 all-gather.6.cloned.1.call-update
  8.6 0.0 reduce-scatter.2.cloned.1.call-start
  8.7 25.9 %all-gather.4.cloned.1.call-done = bf16[128,4096]{1,0:T(8,128)(2,1)} async-done(((bf16[16,4096]{1,0:T(8,128)(2,1)}), bf16[128,4096]{1,0:T(8,128)(2,1)}) %all-gather.4.cloned.1.call-update) | async-done | bytes 1048592 | tf_op jit(solution)/shard_map/all_gather | solution.py:19
  34.6 9.4 %fusion.4 = f32[128,2048]{1,0:T(8,128)} fusion(bf16[128,4096]{1,0:T(8,128)(2,1)} %all-gather.4.cloned.1.call-done, bf16[4096,2048]{1,0:T(8,128)(2,1)} %param.8), kind=kOutput, calls=%fused_computation.16 | convolution fusion | flops 2147483648 | bytes 18874368 | tf_op jit(solution)/shard_map/dot_general | solution.py:22
  44.0 0.0 reduce-scatter.2.cloned.1.call-update
  44.0 46.8 %all-gather.6.cloned.1.call-done = bf16[32,4,4096]{2,1,0:T(4,128)(2,1)} async-done(((bf16[1,4,4096]{2,1,0:T(4,128)(2,1)}), bf16[32,4,4096]{2,1,0:T(4,128)(2,1)}) %all-gather.6.cloned.1.call-update) | async-done | bytes 1048592 | tf_op jit(solution)/shard_map/all_gather | solution.py:34
  90.9 1.3 reshape.25
  92.2 0.2 multiply_reduce_fusion
  92.4 28.9 %reduce-scatter.2.cloned.1.call-done = f32[32,2048]{1,0:T(8,128)} async-done(((f32[128,2048]{1,0:T(8,128)}), f32[32,2048]{1,0:T(8,128)}) %reduce-scatter.2.cloned.1.call-update) | async-done | bytes 262160 | tf_op jit(solution)/shard_map/reduce_scatter | solution.py:21
  121.3 1.1 multiply_reduce_fusion.2
  122.4 16.2 %psum.28 = f32[32]{0:T(128)S(1)} all-reduce(f32[32]{0:T(128)S(1)} %multiply_reduce_fusion.2), channel_id=1, replica_groups=mesh['row'=8,'col'=4] {'row'}, use_global_device_ids=true, to_apply=%region_3.0 | all-reduce | flops 32 | bytes 256 | tf_op jit(solution)/shard_map/psum | solution.py:28
  138.6 1.0 multiply_convert_fusion.2
  139.6 0.7 copy.14
  140.3 3.3 %all-to-all-start = ((bf16[32,4,512]{2,0,1:T(8,128)(2,1)}), bf16[32,4,512]{2,0,1:T(8,128)(2,1)S(1)}, u32[]{:S(2)}, u32[]{:S(2)}) async-start(bf16[32,4,512]{2,0,1:T(8,128)(2,1)} %bitcast.11), calls=%async_computation.1 | async-start | bytes 262144 | tf_op jit(solution)/shard_map/all_to_all | solution.py:33
  143.7 5.0 %all-to-all-done = bf16[32,4,512]{2,0,1:T(8,128)(2,1)S(1)} async-done(((bf16[32,4,512]{2,0,1:T(8,128)(2,1)}), bf16[32,4,512]{2,0,1:T(8,128)(2,1)S(1)}, u32[]{:S(2)}, u32[]{:S(2)}) %all-to-all-start) | async-done | bytes 131104 | tf_op jit(solution)/shard_map/all_to_all | solution.py:33
  148.7 3.7 %multiply_reduce_fusion.1 = (f32[]{:T(128)}, f32[128,512]{1,0:T(8,128)S(1)}) fusion(f32[128,512]{1,0:T(8,128)S(1)} %bitcast.12, bf16[4096,512]{1,0:T(8,128)(2,1)} %param.13, f32[128,4096]{1,0:T(8,128)S(1)} %reshape.25, f32[4096]{0:T(1024)S(1)} %copy-done.2, f32[128]{0:T(128)S(1)} %add_rsqrt_fusion.1), kind=kOutput, calls=%fused_computation.5 | convolution fusion | flops 538640384 | bytes 6832644 | tf_op jit(solution)/shard_map/dot_general | solution.py:37
  152.4 1.5 fusion
  153.9 4.8 %fusion.1 = f32[4096,512]{1,0:T(8,128)} fusion(f32[128,512]{1,0:T(8,128)S(1)} %get-tuple-element.4, f32[128,4096]{1,0:T(8,128)S(1)} %reshape.25, f32[4096]{0:T(1024)S(1)} %copy-done.2, f32[128]{0:T(128)S(1)} %add_rsqrt_fusion.1), kind=kOutput, calls=%fused_computation.11 | convolution fusion | flops 538574848 | bytes 10764800 | tf_op jit(solution)/shard_map/dot_general | solution.py:42
  158.7 37.0 %psum.31 = f32[]{:T(128)} all-reduce(f32[]{:T(128)} %get-tuple-element.3), channel_id=1, replica_groups=mesh['row'=8,'col'=4] {'row','col'}, use_global_device_ids=true, to_apply=%region_8.0 | all-reduce | flops 1 | bytes 8 | tf_op jit(solution)/shard_map/psum | solution.py:40
  195.7 16.4 %psum.29 = f32[4096]{0:T(1024)S(1)} all-reduce(f32[4096]{0:T(1024)S(1)} %fusion), channel_id=1, replica_groups=mesh['row'=8,'col'=4] {'col'}, use_global_device_ids=true, to_apply=%region_5.0 | all-reduce | flops 4096 | bytes 32768 | tf_op jit(solution)/shard_map/psum | solution.py:49
  212.1 26.5 %psum.30 = f32[4096]{0:T(1024)} all-reduce(f32[4096]{0:T(1024)S(1)} %psum.29), channel_id=1, replica_groups=mesh['row'=8,'col'=4] {'row'}, use_global_device_ids=true, to_apply=%region_6.0 | all-reduce | flops 4096 | bytes 32768 | tf_op jit(solution)/shard_map/psum | solution.py:49
  (11 shorter events, 0.1 us)
Async XLA Ops:
  7.2 27.4 %all-gather.4.cloned.1.call-start = ((), (), s32[]{:S(2)}) async-start(), calls=%async_computation.2 | async-start | bytes 1179648 | tf_op jit(solution)/shard_map/all_gather | solution.py:19
  7.9 83.0 %all-gather.6.cloned.1.call-start = ((), (), s32[]{:S(2)}) async-start(), calls=%async_computation.4 | async-start | bytes 1081344 | tf_op jit(solution)/shard_map/all_gather | solution.py:34
  8.6 112.7 %reduce-scatter.2.cloned.1.call-start = ((), (), s32[]{:S(2)}) async-start(), calls=%async_computation.3 | async-start | bytes 1310720 | tf_op jit(solution)/shard_map/reduce_scatter | solution.py:21
  44.0 77.3 %copy-start.1 = (bf16[32,2048]{1,0:T(8,128)(2,1)S(1)}, bf16[32,2048]{1,0:T(8,128)(2,1)}, u32[]{:S(2)}) copy-start(bf16[32,2048]{1,0:T(8,128)(2,1)} %param.9) | copy-start | bytes 393220
  44.0 94.6 %dynamic-slice-start = ((f32[16384]{0:T(1024)}, s32[]{:T(128)}), f32[2048]{0:T(1024)S(1)}, s32[]{:S(2)}) async-start(f32[16384]{0:T(1024)} %param.10, s32[]{:T(128)} %select_n.3), calls=%async_computation.5 | async-start | bytes 16896 | tf_op jit(solution)/shard_map/dynamic_slice | solution.py:29
  92.2 56.5 %copy-start.2 = (f32[4096]{0:T(1024)S(1)}, f32[4096]{0:T(1024)}, u32[]{:S(2)}) copy-start(f32[4096]{0:T(1024)} %param.12) | copy-start | bytes 49156
  140.3 8.3 %all-to-all-start = ((bf16[32,4,512]{2,0,1:T(8,128)(2,1)}), bf16[32,4,512]{2,0,1:T(8,128)(2,1)S(1)}, u32[]{:S(2)}, u32[]{:S(2)}) async-start(bf16[32,4,512]{2,0,1:T(8,128)(2,1)} %bitcast.11), calls=%async_computation.1 | async-start | bytes 262144 | tf_op jit(solution)/shard_map/all_to_all | solution.py:33
  148.7 3.8 %copy-start = (bf16[4096,512]{1,0:T(8,128)(2,1)S(1)}, bf16[4096,512]{1,0:T(8,128)(2,1)}, u32[]{:S(2)}) copy-start(bf16[4096,512]{1,0:T(8,128)(2,1)} %param.13) | copy-start | bytes 12582916
Sparse Core Ops, SparseCore 0:
  9.6 24.9 all-gather.3
  37.6 53.2 all-gather.5
  94.3 26.9 reduce-scatter.1
